TPU v7x, 256 devices: a whole 4x4x8 slice. The times are simulated.
256 devices in a mesh: slide: 16 (over y, x), row: 4 (over z_hi, core), col: 4 (over z_lo).
Axes of the slice: x: 4, y: 4, z: 8 (z_hi: 2, z_lo: 4; z = z_hi * 4 + z_lo), core: 2. Of those that a mesh axis runs over, the one named last changes fastest.
Arguments:
- features: bfloat16 [16, 256, 512, 256], P('slide', 'row', 'col'), may hold values from -6 to 6
- out_grad: bfloat16 [16, 256, 512, 256], P('slide', 'row', 'col'), may hold values from -6 to 6
- depth_weight: bfloat16 [9, 256], replicated, may hold values from -2 to 2
- point_weight: bfloat16 [256, 256], P(('slide', 'row', 'col')), may hold values from -0.375 to 0.375
Outputs:
- feature_grad: bfloat16 [16, 256, 512, 256], P('slide', 'row', 'col')
- point_grad: float32 [256, 256], P(('slide', 'row', 'col'))
- depth_grad: float32 [9, 256], replicated
All inputs are finite; a program needn't handle non-finite values.
Results may differ from a plain program's by a relative error of at most 0.007.
Values may be sent and summed in bfloat16 or wider, within the bound.
No kernel may reach another device: no remote copies, remote signals or barrier semaphores. Data moves between devices by JAX's collectives and lax.ppermute only.
A program may use at most 128 MiB of HBM per device.

v0:
```python
import math
import jax
import jax.numpy as jnp
from jax import lax
from jax.sharding import PartitionSpec as P


def padded(block, sides, width):
    for axis, dim in sides:
        count = lax.axis_size(axis)
        forward = [(i, i + 1) for i in range(count - 1)]
        backward = [(target, source) for source, target in forward]
        low = lax.ppermute(
            lax.slice_in_dim(block, block.shape[dim] - width, None, axis=dim), axis, forward
        )
        high = lax.ppermute(lax.slice_in_dim(block, 0, width, axis=dim), axis, backward)
        block = jnp.concatenate([low, block, high], axis=dim)
    return block


def back_project(grad_flat, point_weight):
    return lax.dot_general(
        grad_flat,
        lax.all_gather(point_weight, ("slide", "row", "col"), axis=0, tiled=True),
        (((1,), (1,)), ((), ())),
        preferred_element_type=jnp.float32,
    ).astype(jnp.bfloat16)


def on_device(features, out_grad, depth_weight, point_weight):
    rows = features.shape[1]
    cols = features.shape[2]
    chans = features.shape[3]
    total = lax.axis_size("slide") * lax.axis_size("row") * lax.axis_size("col") * rows * cols
    scale = 1.0 / math.sqrt(total)
    grad_flat = out_grad[0].reshape(rows * cols, chans)
    feat_pad = padded(features, (("row", 1), ("col", 2)), 2)[0]
    mid_grad = back_project(grad_flat, point_weight).reshape(rows, cols, chans)
    grad_pad = padded(mid_grad[None], (("row", 1), ("col", 2)), 2)[0]
    taps = depth_weight.astype(jnp.float32)
    mid = jnp.zeros((rows, cols, chans), jnp.float32)
    back = jnp.zeros((rows, cols, chans), jnp.float32)
    mid_f = mid_grad.astype(jnp.float32)
    tap_terms = []
    for a in range(3):
        for b in range(3):
            window = feat_pad[2 * a : 2 * a + rows, 2 * b : 2 * b + cols].astype(jnp.float32)
            mid = mid + taps[a * 3 + b] * window
            back = back + taps[a * 3 + b] * grad_pad[
                4 - 2 * a : 4 - 2 * a + rows, 4 - 2 * b : 4 - 2 * b + cols
            ].astype(jnp.float32)
            tap_terms.append(jnp.sum(window * mid_f, axis=(0, 1)))
    mid_flat = mid.astype(jnp.bfloat16).reshape(rows * cols, chans)
    owned = lax.psum_scatter(
        lax.dot_general(
            mid_flat, grad_flat, (((0,), (0,)), ((), ())), preferred_element_type=jnp.float32
        ),
        ("slide", "row", "col"),
        scatter_dimension=0,
        tiled=True,
    )
    depth_grad = lax.psum(jnp.stack(tap_terms), ("slide", "row", "col")) * scale
    feature_grad = back.astype(jnp.bfloat16)[None]
    return (feature_grad, owned * scale, depth_grad)


def solution(mesh):
    placed = (
        P("slide", "row", "col", None),
        P("slide", "row", "col", None),
        P(),
        P(("slide", "row", "col"), None),
    )
    return jax.shard_map(
        on_device,
        mesh=mesh,
        in_specs=placed,
        out_specs=(P("slide", "row", "col", None), P(("slide", "row", "col"), None), P()),
        check_vma=False,
    )
```

profile of v0, /device:TPU:2, one launch (start us, length us, event | category | flops | bytes accessed | tf_op | source)
XLA Modules:
  0.0 971.7 jit_solution(7291026716896225350)
XLA Ops:
  7.2 0.0 copy-start.2
  7.2 0.0 all-reduce.3.cloned.1.call-start
  7.2 1.0 fusion.22
  8.2 0.0 copy-start.3
  8.2 1.7 collective-permute-start.4
  10.0 1.3 collective-permute-start.5
  11.3 0.0 collective-permute-done.4
  11.3 2.5 constant_dynamic-update-slice_fusion.1
  13.8 6.4 collective-permute-done.5
  20.2 0.0 copy-start.1
  20.2 2.1 copy-done.1
  22.3 0.1 fusion.21
  22.4 2.9 collective-permute-start.6
  25.4 1.3 collective-permute-start.7
  26.7 0.0 copy-done.2
  26.7 0.0 copy-done.3
  26.7 585.9 %all-gather = bf16[256,1,256]{2,1,0:T(2,128)(2,1)S(1)} all-gather(bf16[1,1,256]{2,1,0:T(2,128)(2,1)S(1)} %bitcast.71), channel_id=1, replica_groups=mesh['slide'=16,'row'=4,'col'=4] {'slide','row','col'}, dimensions={0}, use_global_device_ids=true | all-gather | bytes 131584 | tf_op jit(solution)/shard_map/all_gather | solution.py:24
  612.6 0.0 collective-permute-done.6
  612.6 0.0 collective-permute-done.7
  612.6 7.2 maximum_bitcast_fusion.1
  619.8 22.3 %fusion.17 = (f32[256]{0:T(256)S(1)}, f32[256]{0:T(256)S(1)}, f32[256]{0:T(256)S(1)}, f32[256]{0:T(256)S(1)}, f32[256]{0:T(256)S(1)}, /*index=5*/f32[256]{0:T(25...) fusion(bf16[68,132,256]{2,1,0:T(8,128)(2,1)} %maximum_bitcast_fusion.1, ...), kind=kOutput, calls=%fused_computation.36 | convolution fusion | flops 1134556928 | bytes 46277632 | tf_op jit(solution)/shard_map/dot_general | solution.py:22
  642.1 0.0 copy-start
  642.1 22.8 %fusion.8 = bf16[64,128,256]{2,1,0:T(8,128)(2,1)S(1)} fusion(f32[256]{0:T(256)S(1)} %bitcast.69, f32[256]{0:T(256)S(1)} %bitcast.67, f32[256]{0:T(256)S(1)} %bitcast.65, f32[256]{0:T(256)S(1)} %bitcast.63, f32[256]{0:T(256)S(1)} %bitcast.61, f32[256]{0:T(256)S(1)} %bitcast.59, f32[256]{0:T(256)S(1)} %bitcast.57, f32[256]{0:T(256)S(1)} %bitcast.55, ...), kind=kLoop, calls=%fused_computation.27 | loop fusion | flops 56623104 | bytes 41952256 | tf_op jit(solution)/shard_map/convert_element_type | solution.py:53
  664.9 0.0 copy-done
  665.0 2.0 fusion.25
  666.9 0.0 all-reduce.3.cloned.1.call-update
  667.0 111.4 %psum.7 = f32[9,256]{1,0:T(8,128)S(1)} all-reduce(f32[9,256]{1,0:T(8,128)S(1)} %stack.39), channel_id=1, replica_groups=mesh['slide'=16,'row'=4,'col'=4] {'slide','row','col'}, use_global_device_ids=true, to_apply=%region_10.0 | all-reduce | flops 2304 | bytes 18432 | tf_op jit(solution)/shard_map/psum | solution.py:62
  778.4 1.0 fusion.23
  779.4 1.7 collective-permute-start
  781.2 1.3 collective-permute-start.1
  782.5 0.6 broadcast_multiply_fusion
  783.1 0.0 collective-permute-done
  783.1 2.5 collective-permute-done.1
  785.6 1.1 pad_maximum_fusion.2
  786.7 4.0 collective-permute-start.2
  790.7 1.3 collective-permute-start.3
  792.0 156.4 %all-reduce.3.cloned.1.call-done = f32[256,256]{1,0:T(8,128)} async-done(((f32[256,256]{1,0:T(8,128)}), f32[256,256]{1,0:T(8,128)}) %all-reduce.3.cloned.1.call-update) | async-done | bytes 262160
  948.4 1.3 dynamic-slice_multiply_fusion
  949.7 0.0 collective-permute-done.2
  949.7 0.0 collective-permute-done.3
  949.7 4.2 maximum_bitcast_fusion
  953.9 10.9 %fusion.18 = bf16[1,64,128,256]{3,2,1,0:T(8,128)(2,1)} fusion(bf16[68,132,256]{2,1,0:T(8,128)(2,1)S(1)} %maximum_bitcast_fusion, f32[256]{0:T(256)S(1)} %bitcast.70, f32[256]{0:T(256)S(1)} %bitcast.68, f32[256]{0:T(256)S(1)} %bitcast.66, f32[256]{0:T(256)S(1)} %bitcast.64, f32[256]{0:T(256)S(1)} %bitcast.62, f32[256]{0:T(256)S(1)} %bitcast.60, ...), kind=kLoop, calls=%fused_computation.40 | loop fusion | flops 56623104 | bytes 41952256 | tf_op jit(solution)/shard_map/broadcast_in_dim | solution.py:63
  (4 shorter events, 0.1 us)
Async XLA Ops:
  7.2 19.5 %copy-start.2 = (bf16[9,256]{1,0:T(8,128)(2,1)S(1)}, bf16[9,256]{1,0:T(8,128)(2,1)}, u32[]{:S(2)}) copy-start(bf16[9,256]{1,0:T(8,128)(2,1)} %param.6) | copy-start | bytes 13828
  7.2 941.2 %all-reduce.3.cloned.1.call-start = ((), (), s32[]{:S(2)}) async-start(), calls=%async_computation | async-start | bytes 524288
  8.2 18.5 %copy-start.3 = (bf16[1,256]{1,0:T(2,128)(2,1)S(1)}, bf16[1,256]{1,0:T(2,128)(2,1)}, u32[]{:S(2)}) copy-start(bf16[1,256]{1,0:T(2,128)(2,1)} %param.7) | copy-start | bytes 1540
  8.2 3.1 collective-permute-start.4
  10.0 10.2 %collective-permute-start.5 = (bf16[1,2,128,256]{3,2,1,0:T(8,128)(2,1)S(1)}, bf16[1,2,128,256]{3,2,1,0:T(8,128)(2,1)S(1)}, u32[]{:S(2)}, u32[]{:S(2)}) collective-permute-start(bf16[1,2,128,256]{3,2,1,0:T(8,128)(2,1)S(1)} %get-tuple-element.16), channel_id=1, source_target_pairs={{4,0},{8,4},{12,8},{5,1},{9,5},{13,9},{6,2},{10,6},{14,10},{7,3},{... | collective-permute-start | bytes 393224 | tf_op jit(solution)/shard_map/ppermute | solution.py:16
  20.2 2.1 copy-start.1
  22.4 590.2 %collective-permute-start.6 = (bf16[1,68,2,256]{3,2,1,0:T(2,128)(2,1)S(1)}, bf16[1,68,2,256]{3,2,1,0:T(2,128)(2,1)S(1)}, u32[]{:S(2)}, u32[]{:S(2)}) collective-permute-start(bf16[1,68,2,256]{3,2,1,0:T(2,128)(2,1)S(1)} %get-tuple-element.12), channel_id=1, source_target_pairs={{0,1},{1,2},{2,3},{4,5},{5,6},{6,7},{8,9},{9,10},{10,11},{12,13},{... | collective-permute-start | bytes 208904 | tf_op jit(solution)/shard_map/ppermute | solution.py:13
  25.4 587.2 %collective-permute-start.7 = (bf16[1,68,2,256]{3,2,1,0:T(2,128)(2,1)S(1)}, bf16[1,68,2,256]{3,2,1,0:T(2,128)(2,1)S(1)}, u32[]{:S(2)}, u32[]{:S(2)}) collective-permute-start(bf16[1,68,2,256]{3,2,1,0:T(2,128)(2,1)S(1)} %get-tuple-element.13), channel_id=1, source_target_pairs={{1,0},{2,1},{3,2},{5,4},{6,5},{7,6},{9,8},{10,9},{11,10},{13,12},{... | collective-permute-start | bytes 208904 | tf_op jit(solution)/shard_map/ppermute | solution.py:16
  642.1 22.8 %copy-start = (bf16[1,64,128,256]{3,2,1,0:T(8,128)(2,1)S(1)}, bf16[1,64,128,256]{3,2,1,0:T(8,128)(2,1)}, u32[]{:S(2)}) copy-start(bf16[1,64,128,256]{3,2,1,0:T(8,128)(2,1)} %param.5) | copy-start | bytes 12582916
  779.4 3.7 collective-permute-start
  781.2 4.4 collective-permute-start.1
  786.7 162.9 %collective-permute-start.2 = (bf16[1,68,2,256]{3,2,1,0:T(2,128)(2,1)S(1)}, bf16[1,68,2,256]{3,2,1,0:T(2,128)(2,1)S(1)}, u32[]{:S(2)}, u32[]{:S(2)}) collective-permute-start(bf16[1,68,2,256]{3,2,1,0:T(2,128)(2,1)S(1)} %get-tuple-element.14), channel_id=1, source_target_pairs={{0,1},{1,2},{2,3},{4,5},{5,6},{6,7},{8,9},{9,10},{10,11},{12,13},{... | collective-permute-start | bytes 208904 | tf_op jit(solution)/shard_map/ppermute | solution.py:13
  790.7 158.9 %collective-permute-start.3 = (bf16[1,68,2,256]{3,2,1,0:T(2,128)(2,1)S(1)}, bf16[1,68,2,256]{3,2,1,0:T(2,128)(2,1)S(1)}, u32[]{:S(2)}, u32[]{:S(2)}) collective-permute-start(bf16[1,68,2,256]{3,2,1,0:T(2,128)(2,1)S(1)} %get-tuple-element.15), channel_id=1, source_target_pairs={{1,0},{2,1},{3,2},{5,4},{6,5},{7,6},{9,8},{10,9},{11,10},{13,12},{... | collective-permute-start | bytes 208904 | tf_op jit(solution)/shard_map/ppermute | solution.py:16
Sparse Core Ops, SparseCore 0:
  667.1 281.2 all-reduce.2
where the time goes:
time: 972 us
  blocking collectives  697 us (72%)
  waiting for transfers between devices  165 us (17%)
  other arithmetic  48.2 us (5%)
  matrix products  24.3 us (2%)
  starting transfers between devices  15.6 us (2%)
  between operations  14.2 us (1%)
    all_gather x1, blocking collectives, back_project(): lax.all_gather(point_weight, ('slide', 'row', 'col'), axis=0, tiled=True)  586 us
    unnamed x2, waiting for transfers between devices  156 us
    psum x1, blocking collectives, on_device(): depth_grad = lax.psum(jnp.stack(tap_terms), ('slide', 'row', 'col')) * scale  111 us
    convert_element_type x1, other arithmetic, on_device(): mid_flat = mid.astype(jnp.bfloat16).reshape(rows * cols, chans)  22.8 us
    dot_general x1, matrix products, back_project(): lax.dot_general(grad_flat, lax.all_gather(point_weight, ('slide', 'row',...  22.3 us
  transfers between devices with their start and end apart: 9, of which 3 were waited for; matrix products, arithmetic and copies ran while one was open for 1% of the time, Pallas kernels for 0%

commit v1 on v0

--- a/solution.py
+++ b/solution.py
@@ -59,7 +59,9 @@
         scatter_dimension=0,
         tiled=True,
     )
-    depth_grad = lax.psum(jnp.stack(tap_terms), ("slide", "row", "col")) * scale
+    depth_grad = (
+        jnp.sum(lax.all_gather(jnp.stack(tap_terms), ("slide", "row", "col")), axis=0) * scale
+    )
     feature_grad = back.astype(jnp.bfloat16)[None]
     return (feature_grad, owned * scale, depth_grad)
 

time: 972 us -> 1630 us (1.68)
  waiting for transfers between devices: 165 us -> 946 us
  blocking collectives: 697 us -> 586 us
    all_gather x0 -> x1, waiting for transfers between devices: none -> 689 us  [on_device(): lax.all_gather(jnp.stack(tap_terms), ('slide', 'row', 'col'))]
    psum x1 -> x0, blocking collectives: 111 us -> none  [on_device(): depth_grad = lax.psum(jnp.stack(tap_terms), ('slide', 'row', 'col')) * scale]
    unnamed x2 -> x3, waiting for transfers between devices: 156 us -> 248 us
  transfers between devices with their start and end apart: 9 -> 10, of which waited for: 3 -> 4; matrix products, arithmetic and copies ran while one was open for 1% -> 3% of each run, Pallas kernels for 0% -> 0%
where the time goes in v1:
time: 1630 us; the launch traced here: 1620 us
  waiting for transfers between devices  946 us (58%)
  blocking collectives  586 us (36%)
  other arithmetic  33.1 us (2%)
  matrix products  24.2 us (1%)
    all_gather x1, waiting for transfers between devices, on_device(): lax.all_gather(jnp.stack(tap_terms), ('slide', 'row', 'col'))  689 us
    all_gather x1, blocking collectives, back_project(): lax.all_gather(point_weight, ('slide', 'row', 'col'), axis=0, tiled=True)  586 us
    unnamed x3, waiting for transfers between devices  248 us
  transfers between devices with their start and end apart: 10, of which 4 were waited for; matrix products, arithmetic and copies ran while one was open for 3% of the time, Pallas kernels for 0%

profile of v1, /device:TPU:2, one launch (start us, length us, event | category | flops | bytes accessed | tf_op | source)
XLA Modules:
  0.0 1621.9 jit_solution(12085309556738057197)
XLA Ops:
  7.2 0.0 copy-start.2
  7.2 0.0 all-reduce.3.cloned.1.call-start
  7.2 1.0 fusion.22
  8.2 0.0 copy-start.3
  8.2 1.7 collective-permute-start.4
  10.0 1.3 collective-permute-start.5
  11.3 0.0 collective-permute-done.4
  11.3 2.5 constant_dynamic-update-slice_fusion.1
  13.8 6.4 collective-permute-done.5
  20.2 0.1 fusion.21
  20.3 2.9 collective-permute-start.6
  23.3 1.3 collective-permute-start.7
  24.6 0.0 copy-done.2
  24.6 0.0 copy-done.3
  24.6 585.9 %all-gather.1 = bf16[256,1,256]{2,1,0:T(2,128)(2,1)S(1)} all-gather(bf16[1,1,256]{2,1,0:T(2,128)(2,1)S(1)} %bitcast.73), channel_id=1, replica_groups=mesh['slide'=16,'row'=4,'col'=4] {'slide','row','col'}, dimensions={0}, use_global_device_ids=true | all-gather | bytes 131584 | tf_op jit(solution)/shard_map/all_gather | solution.py:24
  610.5 0.0 collective-permute-done.6
  610.5 0.0 collective-permute-done.7
  610.5 2.5 maximum_bitcast_fusion.1
  613.0 0.0 copy-start
  613.1 0.0 copy-start.1
  613.1 9.9 fusion.8
  623.0 0.0 copy-done
  623.0 0.0 copy-done.1
  623.0 2.0 fusion.25
  625.0 0.0 all-reduce.3.cloned.1.call-update
  625.1 0.2 all-gather.5.cloned.1.call-start
  625.3 22.2 %fusion.17 = (f32[256]{0:T(256)S(1)}, f32[256]{0:T(256)S(1)}, f32[256]{0:T(256)S(1)}, f32[256]{0:T(256)S(1)}, f32[256]{0:T(256)S(1)}, /*index=5*/f32[256]{0:T(25...) fusion(bf16[68,132,256]{2,1,0:T(8,128)(2,1)} %copy-done, ...), kind=kOutput, calls=%fused_computation.36 | convolution fusion | flops 1134556928 | bytes 46277632 | tf_op jit(solution)/shard_map/dot_general | solution.py:22
  647.4 1.2 stack.39
  648.7 0.0 all-gather.5.cloned.1.call-update
  648.7 1.0 fusion.23
  649.7 1.3 collective-permute-start
  651.0 1.3 collective-permute-start.1
  652.3 0.0 collective-permute-done
  652.3 1.9 collective-permute-done.1
  654.2 1.1 pad_maximum_fusion.2
  655.4 1.3 collective-permute-start.2
  656.7 1.3 collective-permute-start.3
  658.0 248.1 %all-reduce.3.cloned.1.call-done = f32[256,256]{1,0:T(8,128)} async-done(((f32[256,256]{1,0:T(8,128)}), f32[256,256]{1,0:T(8,128)}) %all-reduce.3.cloned.1.call-update) | async-done | bytes 262160
  906.1 1.3 dynamic-slice_multiply_fusion
  907.4 0.0 collective-permute-done.2
  907.4 0.0 collective-permute-done.3
  907.4 4.2 maximum_bitcast_fusion
  911.6 10.9 fusion.18
  922.5 689.4 %all-gather.5.cloned.1.call-done = f32[256,9,256]{2,1,0:T(8,128)} async-done(((f32[1,9,256]{2,1,0:T(8,128)}), f32[256,9,256]{2,1,0:T(8,128)}) %all-gather.5.cloned.1.call-update) | async-done | bytes 2359312 | tf_op jit(solution)/shard_map/all_gather | solution.py:63
  1612.0 2.5 reduce_sum.99
  1614.5 0.6 broadcast_multiply_fusion
  (3 shorter events, 0.0 us)
Async XLA Ops:
  7.2 17.4 %copy-start.2 = (bf16[9,256]{1,0:T(8,128)(2,1)S(1)}, bf16[9,256]{1,0:T(8,128)(2,1)}, u32[]{:S(2)}) copy-start(bf16[9,256]{1,0:T(8,128)(2,1)} %param.6) | copy-start | bytes 13828
  7.2 898.9 %all-reduce.3.cloned.1.call-start = ((), (), s32[]{:S(2)}) async-start(), calls=%async_computation.1 | async-start | bytes 524288
  8.2 16.4 %copy-start.3 = (bf16[1,256]{1,0:T(2,128)(2,1)S(1)}, bf16[1,256]{1,0:T(2,128)(2,1)}, u32[]{:S(2)}) copy-start(bf16[1,256]{1,0:T(2,128)(2,1)} %param.7) | copy-start | bytes 1540
  8.2 3.1 collective-permute-start.4
  10.0 10.2 collective-permute-start.5
  20.3 590.2 %collective-permute-start.6 = (bf16[1,68,2,256]{3,2,1,0:T(2,128)(2,1)S(1)}, bf16[1,68,2,256]{3,2,1,0:T(2,128)(2,1)S(1)}, u32[]{:S(2)}, u32[]{:S(2)}) collective-permute-start(bf16[1,68,2,256]{3,2,1,0:T(2,128)(2,1)S(1)} %get-tuple-element.12), channel_id=1, source_target_pairs={{0,1},{1,2},{2,3},{4,5},{5,6},{6,7},{8,9},{9,10},{10,11},{12,13},{... | collective-permute-start | bytes 208904 | tf_op jit(solution)/shard_map/ppermute | solution.py:13
  23.3 587.2 %collective-permute-start.7 = (bf16[1,68,2,256]{3,2,1,0:T(2,128)(2,1)S(1)}, bf16[1,68,2,256]{3,2,1,0:T(2,128)(2,1)S(1)}, u32[]{:S(2)}, u32[]{:S(2)}) collective-permute-start(bf16[1,68,2,256]{3,2,1,0:T(2,128)(2,1)S(1)} %get-tuple-element.13), channel_id=1, source_target_pairs={{1,0},{2,1},{3,2},{5,4},{6,5},{7,6},{9,8},{10,9},{11,10},{13,12},{... | collective-permute-start | bytes 208904 | tf_op jit(solution)/shard_map/ppermute | solution.py:16
  613.0 10.0 copy-start
  613.1 10.0 copy-start.1
  625.1 986.9 %all-gather.5.cloned.1.call-start = ((), (), s32[]{:S(2)}) async-start(), calls=%async_computation | async-start | bytes 4210688 | tf_op jit(solution)/shard_map/all_gather | solution.py:63
  649.7 2.6 collective-permute-start
  651.0 3.2 collective-permute-start.1
  655.4 252.0 %collective-permute-start.2 = (bf16[1,68,2,256]{3,2,1,0:T(2,128)(2,1)S(1)}, bf16[1,68,2,256]{3,2,1,0:T(2,128)(2,1)S(1)}, u32[]{:S(2)}, u32[]{:S(2)}) collective-permute-start(bf16[1,68,2,256]{3,2,1,0:T(2,128)(2,1)S(1)} %get-tuple-element.14), channel_id=1, source_target_pairs={{0,1},{1,2},{2,3},{4,5},{5,6},{6,7},{8,9},{9,10},{10,11},{12,13},{... | collective-permute-start | bytes 208904 | tf_op jit(solution)/shard_map/ppermute | solution.py:13
  656.7 250.7 %collective-permute-start.3 = (bf16[1,68,2,256]{3,2,1,0:T(2,128)(2,1)S(1)}, bf16[1,68,2,256]{3,2,1,0:T(2,128)(2,1)S(1)}, u32[]{:S(2)}, u32[]{:S(2)}) collective-permute-start(bf16[1,68,2,256]{3,2,1,0:T(2,128)(2,1)S(1)} %get-tuple-element.15), channel_id=1, source_target_pairs={{1,0},{2,1},{3,2},{5,4},{6,5},{7,6},{9,8},{10,9},{11,10},{13,12},{... | collective-permute-start | bytes 208904 | tf_op jit(solution)/shard_map/ppermute | solution.py:16
Sparse Core Ops, SparseCore 0:
  625.2 280.8 all-reduce.2
  908.6 703.3 all-gather.4
